TPU v7x, 32 devices: a whole 2x2x4 slice. The times are simulated.
32 devices in a mesh: gx: 4 (over z), gy: 2 (over x), gz: 4 (over y, core).
Axes of the slice: x: 2, y: 2, z: 4, core: 2. Of those that a mesh axis runs over, the one named last changes fastest.
Arguments:
- loads: float32 [4, 2, 4, 1024, 128], P('gx', 'gy', 'gz'), may hold values from -12 to 12
- start: float32 [4, 2, 4, 1024, 128], P('gx', 'gy', 'gz'), may hold values from -6 to 6
- schur: float32 [4, 2, 4, 1024, 1024], P('gx', 'gy', 'gz'), may hold values from -2 to 8
- inv_local: float32 [4, 2, 4, 1024, 1024], P('gx', 'gy', 'gz'), may hold values from -1 to 3
- basis: float32 [4, 2, 4, 1024, 128], P('gx', 'gy', 'gz'), may hold values from -0.1875 to 0.1875
- coarse_inv: float32 [4096, 4096], P(('gx', 'gy')), may hold values from -0.01 to 0.07
- face_index: int32 [4, 2, 4, 6, 160], P('gx', 'gy', 'gz'), may hold values from 0 to 1023, as said below
- multiplicity: int32 [4, 2, 4, 1024], P('gx', 'gy', 'gz'), may hold values from 1 to 2, as said below
- primal_map: int32 [4, 2, 4, 128], P('gx', 'gy', 'gz'), may hold values from 0 to 4095, all different within a row
Outputs:
- solution: float32 [4, 2, 4, 1024, 128], P('gx', 'gy', 'gz')
- residual: float32 [4, 2, 4, 1024, 128], P('gx', 'gy', 'gz')
Inputs may be any that keep to these rules, and one draw needn't show every extreme that they name: face_index[x, y, z, 2a + s] lists 160 distinct interface slots of subdomain (x, y, z) on its face toward the lower (s = 0) or higher (s = 1) neighbour along grid direction a; the six lists of one subdomain are disjoint. `multiplicity`: 1, plus 1 on slots listed in a face whose neighbouring subdomain lies inside the grid. `primal_map`: each subdomain lists 128 distinct primal unknowns, and every primal unknown is listed by some subdomain.
All inputs are finite; a program needn't handle non-finite values.
Results may differ from a plain program's by a relative error of at most 0.00012.
Values sent between devices are 32-bit elements; how exact they have to be, the bound alone decides.
A program may use at most 64 MiB of HBM per device.

v0:
```python
import jax
import jax.numpy as jnp
from jax import lax
from jax.sharding import PartitionSpec as P

ITERS = 2
damping = 0.6


def extended(block, sides, width):
    for axis, dim in sides:
        count = lax.axis_size(axis)
        forward = [(i, i + 1) for i in range(count - 1)]
        backward = [(target, source) for source, target in forward]
        low = lax.ppermute(
            lax.slice_in_dim(block, block.shape[dim] - width, None, axis=dim), axis, forward
        )
        high = lax.ppermute(lax.slice_in_dim(block, 0, width, axis=dim), axis, backward)
        block = jnp.concatenate([low, block, high], axis=dim)
    return block


def precise(matrix, vectors):
    return jnp.dot(
        matrix, vectors, precision=lax.Precision.HIGHEST, preferred_element_type=jnp.float32
    )


def interface_sum(field, slots):
    face_values = field[slots]
    along_first = extended(face_values[0:2], (("gx", 0),), 1)
    along_second = extended(face_values[2:4], (("gy", 0),), 1)
    along_third = extended(face_values[4:6], (("gz", 0),), 1)
    arrived = jnp.stack(
        [
            along_first[0],
            along_first[3],
            along_second[0],
            along_second[3],
            along_third[0],
            along_third[3],
        ]
    )
    return field.at[slots.reshape(-1)].add(arrived.reshape(-1, field.shape[1]))


def coarse_solve(coarse_rows, coarse_load):
    quarter = coarse_rows.shape[0] // lax.axis_size("gz")
    first_row = lax.axis_index("gz") * quarter
    own_rows = lax.dynamic_slice_in_dim(coarse_rows, first_row, quarter, 0)
    return lax.all_gather(precise(own_rows, coarse_load), ("gx", "gy", "gz"), axis=0, tiled=True)


def body(loads, start, schur, inv_local, basis, coarse_inv, face_index, multiplicity, primal_map):
    unknowns = loads.shape[3]
    load_cases = loads.shape[4]
    load_field = loads.reshape(unknowns, load_cases)
    solution = start.reshape(unknowns, load_cases)
    stiff_matrix = schur.reshape(unknowns, unknowns)
    inverse_matrix = inv_local.reshape(unknowns, unknowns)
    modes = basis.reshape(unknowns, -1)
    slots = face_index.reshape(6, -1)
    weight = 1.0 / multiplicity.reshape(unknowns, 1).astype(jnp.float32)
    primal_ids = primal_map.reshape(-1)
    primal_total = coarse_inv.shape[1]
    residual = solution
    for iteration in range(ITERS):
        residual = load_field - interface_sum(precise(stiff_matrix, solution), slots)
        weighted = weight * residual
        local = precise(inverse_matrix, weighted)
        terms = lax.dot_general(
            modes,
            weighted,
            (((0,), (0,)), ((), ())),
            precision=lax.Precision.HIGHEST,
            preferred_element_type=jnp.float32,
        )
        coarse_local = jnp.zeros((primal_total, load_cases), jnp.float32).at[primal_ids].add(terms)
        coarse_load = lax.psum(coarse_local, ("gx", "gy", "gz"))
        coarse_sol = coarse_solve(coarse_inv, coarse_load)
        correction = precise(modes, coarse_sol[primal_ids])
        update = interface_sum(weight * (local + correction), slots)
        solution = solution + damping * update
    return (solution.reshape(loads.shape), residual.reshape(loads.shape))


def solution(mesh):
    placed = (
        P("gx", "gy", "gz", None, None),
        P("gx", "gy", "gz", None, None),
        P("gx", "gy", "gz", None, None),
        P("gx", "gy", "gz", None, None),
        P("gx", "gy", "gz", None, None),
        P(("gx", "gy"), None),
        P("gx", "gy", "gz", None, None),
        P("gx", "gy", "gz", None),
        P("gx", "gy", "gz", None),
    )
    return jax.shard_map(
        body,
        mesh=mesh,
        in_specs=placed,
        out_specs=(P("gx", "gy", "gz", None, None), P("gx", "gy", "gz", None, None)),
        check_vma=False,
    )
```

profile of v0, /device:TPU:11, one launch (start us, length us, event | category | flops | bytes accessed | tf_op | source)
XLA Modules:
  0.0 563.9 jit_solution(8171522895181699997)
XLA Ops:
  8.1 5.3 fusion.6
  22.9 4.0 collective-permute-start.3
  26.9 4.8 collective-permute-start.4
  34.0 3.7 collective-permute-done.5
  37.8 6.3 %scatter_fusion = f32[1024,128]{1,0:T(8,128)S(1)} fusion(f32[1024,128]{1,0:T(8,128)S(1)} %fusion.6, s32[960]{0:T(1024)S(1)} %bitcast.137, f32[960,128]{1,0:T(8,128)S(1)} %bitcast.133), kind=kCustom, calls=%fused_computation.6 | custom fusion | flops 122880 | bytes 1478400 | tf_op jit(solution)/shard_map/scatter-add | solution.py:44
  47.7 132.7 %all-reduce.3.cloned.1.call-done = f32[4096,128]{1,0:T(8,128)} async-done(((f32[4096,128]{1,0:T(8,128)}), f32[4096,128]{1,0:T(8,128)}) %all-reduce.3.cloned.1.call-update) | async-done | bytes 2097168 | tf_op jit(solution)/shard_map/psum | solution.py:79
  180.4 5.0 fusion.10
  185.9 55.8 %all-gather.3.cloned.1.call-done = f32[4096,128]{1,0:T(8,128)} async-done(((f32[128,128]{1,0:T(8,128)}), f32[4096,128]{1,0:T(8,128)}) %all-gather.3.cloned.1.call-update) | async-done | bytes 2097168 | tf_op jit(solution)/shard_map/all_gather | solution.py:51
  244.6 6.0 %fusion.27 = f32[1024,128]{0,1:T(8,128)S(1)} fusion(f32[128,1024]{1,0:T(8,128)S(1)} %fusion.40, f32[1,1,1,1024,1024]{4,3,2,1,0:T(8,128)} %param.12, f32[1024]{0:T(1024)S(1)} %bitcast.142, f32[1024,128]{1,0:T(8,128)S(1)} %scatter_fusion, f32[1,1,1,1024,128]{4,3,2,1,0:T(8,128)S(1)} %copy-done.1), kind=kOutput, calls=%fused_computation.29 | convolution fusion | flops 1611137024 | bytes 6295552 | tf_op jit(solution)/shard_map/dot_general | solution.py:24
  260.3 4.0 collective-permute-start.9
  270.1 3.7 collective-permute-done.11
  273.8 6.3 %scatter_fusion.1 = f32[1024,128]{1,0:T(8,128)S(1)} fusion(f32[1024,128]{1,0:T(8,128)S(1)} %copy.12, s32[960]{0:T(1024)S(1)} %bitcast.138, f32[960,128]{1,0:T(8,128)S(1)} %bitcast.134), kind=kCustom, calls=%fused_computation.8 | custom fusion | flops 122880 | bytes 1478400 | tf_op jit(solution)/shard_map/scatter-add | solution.py:44
  280.1 6.7 %fusion.30 = f32[1024,128]{0,1:T(8,128)S(1)} fusion(f32[1,1,1,1024,1024]{4,3,2,1,0:T(8,128)} %param.11, f32[1,1,1,1024,128]{4,3,2,1,0:T(8,128)S(1)} %copy-done.2, f32[1024,128]{1,0:T(8,128)S(1)} %scatter_fusion.1), kind=kOutput, calls=%fused_computation.30 | convolution fusion | flops 1610874880 | bytes 5767168 | tf_op jit(solution)/shard_map/dot_general | solution.py:24
  296.5 4.0 collective-permute-start.15
  305.7 3.7 collective-permute-done.17
  309.4 6.2 %scatter_fusion.2 = f32[1024,128]{1,0:T(8,128)S(1)} fusion(f32[1024,128]{1,0:T(8,128)S(1)} %copy.14, s32[960]{0:T(1024)S(1)} %bitcast.139, f32[960,128]{1,0:T(8,128)S(1)} %bitcast.135), kind=kCustom, calls=%fused_computation.9 | custom fusion | flops 122880 | bytes 1478400 | tf_op jit(solution)/shard_map/scatter-add | solution.py:44
  319.3 132.1 %all-reduce.5.cloned.1.call-done = f32[4096,128]{1,0:T(8,128)} async-done(((f32[4096,128]{1,0:T(8,128)}), f32[4096,128]{1,0:T(8,128)}) %all-reduce.5.cloned.1.call-update) | async-done | bytes 2097168 | tf_op jit(solution)/shard_map/psum | solution.py:79
  451.4 5.0 fusion.8
  456.4 56.3 %all-gather.5.cloned.1.call-done = f32[4096,128]{1,0:T(8,128)} async-done(((f32[128,128]{1,0:T(8,128)}), f32[4096,128]{1,0:T(8,128)}) %all-gather.5.cloned.1.call-update) | async-done | bytes 2097168 | tf_op jit(solution)/shard_map/all_gather | solution.py:51
  515.6 6.8 %fusion.21 = f32[1024,128]{0,1:T(8,128)} fusion(f32[128,1024]{1,0:T(8,128)S(1)} %fusion.37, f32[1,1,1,1024,1024]{4,3,2,1,0:T(8,128)} %param.12, f32[1024]{0:T(1024)S(1)} %bitcast.144, f32[1024,128]{1,0:T(8,128)S(1)} %scatter_fusion.2, f32[1,1,1,1024,128]{4,3,2,1,0:T(8,128)S(1)} %copy-done.1), kind=kOutput, calls=%fused_computation.27 | convolution fusion | flops 1611137024 | bytes 6295552 | tf_op jit(solution)/shard_map/dot_general | solution.py:24
  523.7 4.0 gather_fusion.5
  536.3 4.2 collective-permute-start.21
  546.3 3.7 collective-permute-done.23
  550.0 6.2 %scatter_fusion.3 = f32[1024,128]{1,0:T(8,128)S(1)} fusion(f32[1024,128]{1,0:T(8,128)S(1)} %copy.16, s32[960]{0:T(1024)S(1)} %bitcast.140, f32[960,128]{1,0:T(8,128)S(1)} %bitcast.136), kind=kCustom, calls=%fused_computation.11 | custom fusion | flops 122880 | bytes 1478400 | tf_op jit(solution)/shard_map/scatter-add | solution.py:44
  (112 shorter events, 72.6 us)
Async XLA Ops:
  7.2 173.2 %all-reduce.3.cloned.1.call-start = ((), (), s32[]{:S(2)}) async-start(), calls=%async_computation | async-start | bytes 4194304 | tf_op jit(solution)/shard_map/psum | solution.py:79
  16.4 15.6 %collective-permute-start = (f32[1,160,128]{2,1,0:T(8,128)S(1)}, f32[1,160,128]{2,1,0:T(8,128)S(1)}, u32[]{:S(2)}, u32[]{:S(2)}) collective-permute-start(f32[1,160,128]{2,1,0:T(8,128)S(1)} %get-tuple-element.25), channel_id=1, source_target_pairs={{0,8},{8,16},{16,24},{1,9},{9,17},{17,25},{2,10},{10,18},{18,26},{... | collective-permute-start | bytes 245768 | tf_op jit(solution)/shard_map/ppermute | solution.py:15
  19.6 14.4 %collective-permute-start.1 = (f32[1,160,128]{2,1,0:T(8,128)S(1)}, f32[1,160,128]{2,1,0:T(8,128)S(1)}, u32[]{:S(2)}, u32[]{:S(2)}) collective-permute-start(f32[1,160,128]{2,1,0:T(8,128)S(1)} %get-tuple-element.24), channel_id=1, source_target_pairs={{8,0},{16,8},{24,16},{9,1},{17,9},{25,17},{10,2},{18,10},{26,18},{... | collective-permute-start | bytes 245768 | tf_op jit(solution)/shard_map/ppermute | solution.py:18
  21.6 12.3 %collective-permute-start.2 = (f32[1,160,128]{2,1,0:T(8,128)S(1)}, f32[1,160,128]{2,1,0:T(8,128)S(1)}, u32[]{:S(2)}, u32[]{:S(2)}) collective-permute-start(f32[1,160,128]{2,1,0:T(8,128)S(1)} %get-tuple-element.23), channel_id=1, source_target_pairs={{0,4},{1,5},{2,6},{3,7},{8,12},{9,13},{10,14},{11,15},{16,20},{17,... | collective-permute-start | bytes 245768 | tf_op jit(solution)/shard_map/ppermute | solution.py:15
  22.9 11.0 %collective-permute-start.3 = (f32[1,160,128]{2,1,0:T(8,128)S(1)}, f32[1,160,128]{2,1,0:T(8,128)S(1)}, u32[]{:S(2)}, u32[]{:S(2)}) collective-permute-start(f32[1,160,128]{2,1,0:T(8,128)S(1)} %get-tuple-element.22), channel_id=1, source_target_pairs={{4,0},{5,1},{6,2},{7,3},{12,8},{13,9},{14,10},{15,11},{20,16},{21,... | collective-permute-start | bytes 245768 | tf_op jit(solution)/shard_map/ppermute | solution.py:18
  26.9 7.1 %collective-permute-start.4 = (f32[1,160,128]{2,1,0:T(8,128)S(1)}, f32[1,160,128]{2,1,0:T(8,128)S(1)}, u32[]{:S(2)}, u32[]{:S(2)}) collective-permute-start(f32[1,160,128]{2,1,0:T(8,128)S(1)} %get-tuple-element.21), channel_id=1, source_target_pairs={{0,1},{1,2},{2,3},{4,5},{5,6},{6,7},{8,9},{9,10},{10,11},{12,13},{... | collective-permute-start | bytes 245768 | tf_op jit(solution)/shard_map/ppermute | solution.py:15
  32.0 5.8 %collective-permute-start.5 = (f32[1,160,128]{2,1,0:T(8,128)S(1)}, f32[1,160,128]{2,1,0:T(8,128)S(1)}, u32[]{:S(2)}, u32[]{:S(2)}) collective-permute-start(f32[1,160,128]{2,1,0:T(8,128)S(1)} %get-tuple-element.20), channel_id=1, source_target_pairs={{1,0},{2,1},{3,2},{5,4},{6,5},{7,6},{9,8},{10,9},{11,10},{13,12},{... | collective-permute-start | bytes 245768 | tf_op jit(solution)/shard_map/ppermute | solution.py:18
  47.6 194.0 %all-gather.3.cloned.1.call-start = ((), (), s32[]{:S(2)}) async-start(), calls=%async_computation.1 | async-start | bytes 2162688 | tf_op jit(solution)/shard_map/all_gather | solution.py:51
  185.4 266.1 %all-reduce.5.cloned.1.call-start = ((), (), s32[]{:S(2)}) async-start(), calls=%async_computation.2 | async-start | bytes 4194304 | tf_op jit(solution)/shard_map/psum | solution.py:79
  253.7 14.3 %collective-permute-start.6 = (f32[1,160,128]{2,1,0:T(8,128)S(1)}, f32[1,160,128]{2,1,0:T(8,128)S(1)}, u32[]{:S(2)}, u32[]{:S(2)}) collective-permute-start(f32[1,160,128]{2,1,0:T(8,128)S(1)} %get-tuple-element.19), channel_id=1, source_target_pairs={{0,8},{8,16},{16,24},{1,9},{9,17},{17,25},{2,10},{10,18},{18,26},{... | collective-permute-start | bytes 245768 | tf_op jit(solution)/shard_map/ppermute | solution.py:15
  256.1 13.9 %collective-permute-start.7 = (f32[1,160,128]{2,1,0:T(8,128)S(1)}, f32[1,160,128]{2,1,0:T(8,128)S(1)}, u32[]{:S(2)}, u32[]{:S(2)}) collective-permute-start(f32[1,160,128]{2,1,0:T(8,128)S(1)} %get-tuple-element.18), channel_id=1, source_target_pairs={{8,0},{16,8},{24,16},{9,1},{17,9},{25,17},{10,2},{18,10},{26,18},{... | collective-permute-start | bytes 245768 | tf_op jit(solution)/shard_map/ppermute | solution.py:18
  259.0 11.0 %collective-permute-start.8 = (f32[1,160,128]{2,1,0:T(8,128)S(1)}, f32[1,160,128]{2,1,0:T(8,128)S(1)}, u32[]{:S(2)}, u32[]{:S(2)}) collective-permute-start(f32[1,160,128]{2,1,0:T(8,128)S(1)} %get-tuple-element.17), channel_id=1, source_target_pairs={{0,4},{1,5},{2,6},{3,7},{8,12},{9,13},{10,14},{11,15},{16,20},{17,... | collective-permute-start | bytes 245768 | tf_op jit(solution)/shard_map/ppermute | solution.py:15
  260.3 9.7 %collective-permute-start.9 = (f32[1,160,128]{2,1,0:T(8,128)S(1)}, f32[1,160,128]{2,1,0:T(8,128)S(1)}, u32[]{:S(2)}, u32[]{:S(2)}) collective-permute-start(f32[1,160,128]{2,1,0:T(8,128)S(1)} %get-tuple-element.16), channel_id=1, source_target_pairs={{4,0},{5,1},{6,2},{7,3},{12,8},{13,9},{14,10},{15,11},{20,16},{21,... | collective-permute-start | bytes 245768 | tf_op jit(solution)/shard_map/ppermute | solution.py:18
  268.0 5.8 %collective-permute-start.11 = (f32[1,160,128]{2,1,0:T(8,128)S(1)}, f32[1,160,128]{2,1,0:T(8,128)S(1)}, u32[]{:S(2)}, u32[]{:S(2)}) collective-permute-start(f32[1,160,128]{2,1,0:T(8,128)S(1)} %get-tuple-element.14), channel_id=1, source_target_pairs={{1,0},{2,1},{3,2},{5,4},{6,5},{7,6},{9,8},{10,9},{11,10},{13,12},{... | collective-permute-start | bytes 245768 | tf_op jit(solution)/shard_map/ppermute | solution.py:18
  289.9 13.7 %collective-permute-start.12 = (f32[1,160,128]{2,1,0:T(8,128)S(1)}, f32[1,160,128]{2,1,0:T(8,128)S(1)}, u32[]{:S(2)}, u32[]{:S(2)}) collective-permute-start(f32[1,160,128]{2,1,0:T(8,128)S(1)} %get-tuple-element.13), channel_id=1, source_target_pairs={{0,8},{8,16},{16,24},{1,9},{9,17},{17,25},{2,10},{10,18},{18,26},{... | collective-permute-start | bytes 245768 | tf_op jit(solution)/shard_map/ppermute | solution.py:15
  292.4 13.1 %collective-permute-start.13 = (f32[1,160,128]{2,1,0:T(8,128)S(1)}, f32[1,160,128]{2,1,0:T(8,128)S(1)}, u32[]{:S(2)}, u32[]{:S(2)}) collective-permute-start(f32[1,160,128]{2,1,0:T(8,128)S(1)} %get-tuple-element.12), channel_id=1, source_target_pairs={{8,0},{16,8},{24,16},{9,1},{17,9},{25,17},{10,2},{18,10},{26,18},{... | collective-permute-start | bytes 245768 | tf_op jit(solution)/shard_map/ppermute | solution.py:18
  295.2 10.4 %collective-permute-start.14 = (f32[1,160,128]{2,1,0:T(8,128)S(1)}, f32[1,160,128]{2,1,0:T(8,128)S(1)}, u32[]{:S(2)}, u32[]{:S(2)}) collective-permute-start(f32[1,160,128]{2,1,0:T(8,128)S(1)} %get-tuple-element.11), channel_id=1, source_target_pairs={{0,4},{1,5},{2,6},{3,7},{8,12},{9,13},{10,14},{11,15},{16,20},{17,... | collective-permute-start | bytes 245768 | tf_op jit(solution)/shard_map/ppermute | solution.py:15
  296.5 9.2 %collective-permute-start.15 = (f32[1,160,128]{2,1,0:T(8,128)S(1)}, f32[1,160,128]{2,1,0:T(8,128)S(1)}, u32[]{:S(2)}, u32[]{:S(2)}) collective-permute-start(f32[1,160,128]{2,1,0:T(8,128)S(1)} %get-tuple-element.10), channel_id=1, source_target_pairs={{4,0},{5,1},{6,2},{7,3},{12,8},{13,9},{14,10},{15,11},{20,16},{21,... | collective-permute-start | bytes 245768 | tf_op jit(solution)/shard_map/ppermute | solution.py:18
  303.6 5.8 %collective-permute-start.17 = (f32[1,160,128]{2,1,0:T(8,128)S(1)}, f32[1,160,128]{2,1,0:T(8,128)S(1)}, u32[]{:S(2)}, u32[]{:S(2)}) collective-permute-start(f32[1,160,128]{2,1,0:T(8,128)S(1)} %get-tuple-element.8), channel_id=1, source_target_pairs={{1,0},{2,1},{3,2},{5,4},{6,5},{7,6},{9,8},{10,9},{11,10},{13,12},{... | collective-permute-start | bytes 245768 | tf_op jit(solution)/shard_map/ppermute | solution.py:18
  319.2 193.5 %all-gather.5.cloned.1.call-start = ((), (), s32[]{:S(2)}) async-start(), calls=%async_computation.3 | async-start | bytes 2162688 | tf_op jit(solution)/shard_map/all_gather | solution.py:51
  528.8 15.4 %collective-permute-start.18 = (f32[1,160,128]{2,1,0:T(8,128)S(1)}, f32[1,160,128]{2,1,0:T(8,128)S(1)}, u32[]{:S(2)}, u32[]{:S(2)}) collective-permute-start(f32[1,160,128]{2,1,0:T(8,128)S(1)} %get-tuple-element.7), channel_id=1, source_target_pairs={{0,8},{8,16},{16,24},{1,9},{9,17},{17,25},{2,10},{10,18},{18,26},{... | collective-permute-start | bytes 245768 | tf_op jit(solution)/shard_map/ppermute | solution.py:15
  532.1 14.1 %collective-permute-start.19 = (f32[1,160,128]{2,1,0:T(8,128)S(1)}, f32[1,160,128]{2,1,0:T(8,128)S(1)}, u32[]{:S(2)}, u32[]{:S(2)}) collective-permute-start(f32[1,160,128]{2,1,0:T(8,128)S(1)} %get-tuple-element.6), channel_id=1, source_target_pairs={{8,0},{16,8},{24,16},{9,1},{17,9},{25,17},{10,2},{18,10},{26,18},{... | collective-permute-start | bytes 245768 | tf_op jit(solution)/shard_map/ppermute | solution.py:18
  535.0 11.2 %collective-permute-start.20 = (f32[1,160,128]{2,1,0:T(8,128)S(1)}, f32[1,160,128]{2,1,0:T(8,128)S(1)}, u32[]{:S(2)}, u32[]{:S(2)}) collective-permute-start(f32[1,160,128]{2,1,0:T(8,128)S(1)} %get-tuple-element.5), channel_id=1, source_target_pairs={{0,4},{1,5},{2,6},{3,7},{8,12},{9,13},{10,14},{11,15},{16,20},{17,... | collective-permute-start | bytes 245768 | tf_op jit(solution)/shard_map/ppermute | solution.py:15
  536.3 9.9 %collective-permute-start.21 = (f32[1,160,128]{2,1,0:T(8,128)S(1)}, f32[1,160,128]{2,1,0:T(8,128)S(1)}, u32[]{:S(2)}, u32[]{:S(2)}) collective-permute-start(f32[1,160,128]{2,1,0:T(8,128)S(1)} %get-tuple-element.4), channel_id=1, source_target_pairs={{4,0},{5,1},{6,2},{7,3},{12,8},{13,9},{14,10},{15,11},{20,16},{21,... | collective-permute-start | bytes 245768 | tf_op jit(solution)/shard_map/ppermute | solution.py:18
  (10 other events, 127.3 us)
Sparse Core Ops, SparseCore 0:
  47.8 132.5 all-reduce.2
  185.5 56.1 all-gather.2
  319.4 132.0 all-reduce.4
  456.6 56.1 all-gather.4
where the time goes:
time: 572 us; the launch traced here: 564 us
  waiting for transfers between devices  392 us (69%)
  starting transfers between devices  66.1 us (12%)
  matrix products  38.4 us (7%)
  other arithmetic  32.4 us (6%)
  local copies, waits for them, and re-layouts  20.3 us (4%)
  between operations  14.8 us (3%)
    psum x2, waiting for transfers between devices, body(): coarse_load = lax.psum(coarse_local, ('gx', 'gy', 'gz'))  265 us
    all_gather x2, waiting for transfers between devices, coarse_solve(): lax.all_gather(precise(own_rows, coarse_load), ('gx', 'gy', 'gz'), axis=0...  112 us
    dot_general x8, matrix products, precise(): jnp.dot(matrix, vectors, precision=lax.Precision.HIGHEST, preferred_eleme...  36 us
    ppermute x12, starting transfers between devices, extended(): lax.ppermute(lax.slice_in_dim(block, 0, width, axis=dim), axis, backward)  34.5 us
    ppermute x12, starting transfers between devices, extended(): lax.ppermute(lax.slice_in_dim(block, block.shape[dim] - width, None, axis...  31 us
    scatter-add x4, other arithmetic, interface_sum(): return field.at[slots.reshape(-1)].add(arrived.reshape(-1, field.shape[1]))  25 us
    ppermute x12, waiting for transfers between devices, extended(): lax.ppermute(lax.slice_in_dim(block, 0, width, axis=dim), axis, backward)  14.9 us
    gather x4, local copies, waits for them, and re-layouts, interface_sum(): face_values = field[slots]  12.7 us
  transfers between devices with their start and end apart: 28, of which 8 were waited for; matrix products, arithmetic and copies ran while one was open for 0% of the time, Pallas kernels for 0%

commit v1 on v0

--- a/solution.py
+++ b/solution.py
@@ -76,7 +76,7 @@
             preferred_element_type=jnp.float32,
         )
         coarse_local = jnp.zeros((primal_total, load_cases), jnp.float32).at[primal_ids].add(terms)
-        coarse_load = lax.psum(coarse_local, ("gx", "gy", "gz"))
+        coarse_load = lax.psum(lax.psum(coarse_local, ("gy", "gz")), "gx")
         coarse_sol = coarse_solve(coarse_inv, coarse_load)
         correction = precise(modes, coarse_sol[primal_ids])
         update = interface_sum(weight * (local + correction), slots)

time: 572 us -> 602 us (1.052)
  waiting for transfers between devices: 392 us -> 422 us
    psum x2 -> x4, waiting for transfers between devices: 265 us -> 294 us  [body(): coarse_load = lax.psum(lax.psum(coarse_local, ('gy', 'gz')), 'gx')]
  transfers between devices with their start and end apart: 28 -> 30, of which waited for: 8 -> 10; matrix products, arithmetic and copies ran while one was open for 0% -> 0% of each run, Pallas kernels for 0% -> 0%
where the time goes in v1:
time: 602 us; the launch traced here: 594 us
  waiting for transfers between devices  422 us (70%)
  starting transfers between devices  66.2 us (11%)
  matrix products  38.4 us (6%)
  other arithmetic  32.4 us (5%)
  local copies, waits for them, and re-layouts  20.3 us (3%)
  between operations  15.1 us (3%)
    psum x4, waiting for transfers between devices, body(): coarse_load = lax.psum(lax.psum(coarse_local, ('gy', 'gz')), 'gx')  294 us
    all_gather x2, waiting for transfers between devices, coarse_solve(): lax.all_gather(precise(own_rows, coarse_load), ('gx', 'gy', 'gz'), axis=0...  112 us
    dot_general x8, matrix products, precise(): jnp.dot(matrix, vectors, precision=lax.Precision.HIGHEST, preferred_eleme...  36 us
    ppermute x12, starting transfers between devices, extended(): lax.ppermute(lax.slice_in_dim(block, 0, width, axis=dim), axis, backward)  34.3 us
    ppermute x12, starting transfers between devices, extended(): lax.ppermute(lax.slice_in_dim(block, block.shape[dim] - width, None, axis...  31.3 us
    scatter-add x4, other arithmetic, interface_sum(): return field.at[slots.reshape(-1)].add(arrived.reshape(-1, field.shape[1]))  25 us
    ppermute x12, waiting for transfers between devices, extended(): lax.ppermute(lax.slice_in_dim(block, 0, width, axis=dim), axis, backward)  14.9 us
    gather x4, local copies, waits for them, and re-layouts, interface_sum(): face_values = field[slots]  12.7 us
  transfers between devices with their start and end apart: 30, of which 10 were waited for; matrix products, arithmetic and copies ran while one was open for 0% of the time, Pallas kernels for 0%

profile of v1, /device:TPU:11, one launch (start us, length us, event | category | flops | bytes accessed | tf_op | source)
XLA Modules:
  0.0 594.0 jit_solution(2717623366845315560)
XLA Ops:
  8.1 5.3 fusion.6
  22.9 4.0 collective-permute-start.3
  26.9 4.8 collective-permute-start.4
  34.0 3.7 collective-permute-done.5
  37.8 6.3 %scatter_fusion = f32[1024,128]{1,0:T(8,128)S(1)} fusion(f32[1024,128]{1,0:T(8,128)S(1)} %fusion.6, s32[960]{0:T(1024)S(1)} %bitcast.137, f32[960,128]{1,0:T(8,128)S(1)} %bitcast.133), kind=kCustom, calls=%fused_computation.6 | custom fusion | flops 122880 | bytes 1478400 | tf_op jit(solution)/shard_map/scatter-add | solution.py:44
  47.7 59.9 %all-reduce.5.cloned.1.call-done = f32[4096,128]{1,0:T(8,128)} async-done(((f32[4096,128]{1,0:T(8,128)}), f32[4096,128]{1,0:T(8,128)}) %all-reduce.5.cloned.1.call-update) | async-done | bytes 2097168 | tf_op jit(solution)/shard_map/psum | solution.py:79
  107.7 87.6 %all-reduce.7.cloned.1.call-done = f32[4096,128]{1,0:T(8,128)} async-done(((f32[4096,128]{1,0:T(8,128)}), f32[4096,128]{1,0:T(8,128)}) %all-reduce.7.cloned.1.call-update) | async-done | bytes 2097168 | tf_op jit(solution)/shard_map/psum | solution.py:79
  195.2 5.0 fusion.10
  200.8 55.9 %all-gather.3.cloned.1.call-done = f32[4096,128]{1,0:T(8,128)} async-done(((f32[128,128]{1,0:T(8,128)}), f32[4096,128]{1,0:T(8,128)}) %all-gather.3.cloned.1.call-update) | async-done | bytes 2097168 | tf_op jit(solution)/shard_map/all_gather | solution.py:51
  259.6 6.0 %fusion.27 = f32[1024,128]{0,1:T(8,128)S(1)} fusion(f32[128,1024]{1,0:T(8,128)S(1)} %fusion.40, f32[1,1,1,1024,1024]{4,3,2,1,0:T(8,128)} %param.12, f32[1024]{0:T(1024)S(1)} %bitcast.142, f32[1024,128]{1,0:T(8,128)S(1)} %scatter_fusion, f32[1,1,1,1024,128]{4,3,2,1,0:T(8,128)S(1)} %copy-done.1), kind=kOutput, calls=%fused_computation.29 | convolution fusion | flops 1611137024 | bytes 6295552 | tf_op jit(solution)/shard_map/dot_general | solution.py:24
  275.3 4.0 collective-permute-start.9
  285.1 3.7 collective-permute-done.11
  288.8 6.3 %scatter_fusion.1 = f32[1024,128]{1,0:T(8,128)S(1)} fusion(f32[1024,128]{1,0:T(8,128)S(1)} %copy.12, s32[960]{0:T(1024)S(1)} %bitcast.138, f32[960,128]{1,0:T(8,128)S(1)} %bitcast.134), kind=kCustom, calls=%fused_computation.8 | custom fusion | flops 122880 | bytes 1478400 | tf_op jit(solution)/shard_map/scatter-add | solution.py:44
  295.1 6.7 %fusion.30 = f32[1024,128]{0,1:T(8,128)S(1)} fusion(f32[1,1,1,1024,1024]{4,3,2,1,0:T(8,128)} %param.11, f32[1,1,1,1024,128]{4,3,2,1,0:T(8,128)S(1)} %copy-done.2, f32[1024,128]{1,0:T(8,128)S(1)} %scatter_fusion.1), kind=kOutput, calls=%fused_computation.30 | convolution fusion | flops 1610874880 | bytes 5767168 | tf_op jit(solution)/shard_map/dot_general | solution.py:24
  311.5 4.0 collective-permute-start.15
  324.4 6.2 %scatter_fusion.2 = f32[1024,128]{1,0:T(8,128)S(1)} fusion(f32[1024,128]{1,0:T(8,128)S(1)} %copy.14, s32[960]{0:T(1024)S(1)} %bitcast.139, f32[960,128]{1,0:T(8,128)S(1)} %bitcast.135), kind=kCustom, calls=%fused_computation.9 | custom fusion | flops 122880 | bytes 1478400 | tf_op jit(solution)/shard_map/scatter-add | solution.py:44
  334.3 59.4 %all-reduce.9.cloned.1.call-done = f32[4096,128]{1,0:T(8,128)} async-done(((f32[4096,128]{1,0:T(8,128)}), f32[4096,128]{1,0:T(8,128)}) %all-reduce.9.cloned.1.call-update) | async-done | bytes 2097168 | tf_op jit(solution)/shard_map/psum | solution.py:79
  393.7 87.4 %all-reduce.11.cloned.1.call-done = f32[4096,128]{1,0:T(8,128)} async-done(((f32[4096,128]{1,0:T(8,128)}), f32[4096,128]{1,0:T(8,128)}) %all-reduce.11.cloned.1.call-update) | async-done | bytes 2097168 | tf_op jit(solution)/shard_map/psum | solution.py:79
  481.1 5.0 fusion.8
  486.1 56.4 %all-gather.5.cloned.1.call-done = f32[4096,128]{1,0:T(8,128)} async-done(((f32[128,128]{1,0:T(8,128)}), f32[4096,128]{1,0:T(8,128)}) %all-gather.5.cloned.1.call-update) | async-done | bytes 2097168 | tf_op jit(solution)/shard_map/all_gather | solution.py:51
  545.5 6.8 %fusion.21 = f32[1024,128]{0,1:T(8,128)} fusion(f32[128,1024]{1,0:T(8,128)S(1)} %fusion.37, f32[1,1,1,1024,1024]{4,3,2,1,0:T(8,128)} %param.12, f32[1024]{0:T(1024)S(1)} %bitcast.144, f32[1024,128]{1,0:T(8,128)S(1)} %scatter_fusion.2, f32[1,1,1,1024,128]{4,3,2,1,0:T(8,128)S(1)} %copy-done.1), kind=kOutput, calls=%fused_computation.27 | convolution fusion | flops 1611137024 | bytes 6295552 | tf_op jit(solution)/shard_map/dot_general | solution.py:24
  553.5 4.0 gather_fusion.5
  566.3 4.0 collective-permute-start.21
  579.8 6.2 %scatter_fusion.3 = f32[1024,128]{1,0:T(8,128)S(1)} fusion(f32[1024,128]{1,0:T(8,128)S(1)} %copy.16, s32[960]{0:T(1024)S(1)} %bitcast.140, f32[960,128]{1,0:T(8,128)S(1)} %bitcast.136), kind=kCustom, calls=%fused_computation.11 | custom fusion | flops 122880 | bytes 1478400 | tf_op jit(solution)/shard_map/scatter-add | solution.py:44
  (118 shorter events, 80.3 us)
Async XLA Ops:
  7.2 100.4 %all-reduce.5.cloned.1.call-start = ((), (), s32[]{:S(2)}) async-start(), calls=%async_computation | async-start | bytes 4194304 | tf_op jit(solution)/shard_map/psum | solution.py:79
  16.4 15.6 %collective-permute-start = (f32[1,160,128]{2,1,0:T(8,128)S(1)}, f32[1,160,128]{2,1,0:T(8,128)S(1)}, u32[]{:S(2)}, u32[]{:S(2)}) collective-permute-start(f32[1,160,128]{2,1,0:T(8,128)S(1)} %get-tuple-element.25), channel_id=1, source_target_pairs={{0,8},{8,16},{16,24},{1,9},{9,17},{17,25},{2,10},{10,18},{18,26},{... | collective-permute-start | bytes 245768 | tf_op jit(solution)/shard_map/ppermute | solution.py:15
  19.6 14.4 %collective-permute-start.1 = (f32[1,160,128]{2,1,0:T(8,128)S(1)}, f32[1,160,128]{2,1,0:T(8,128)S(1)}, u32[]{:S(2)}, u32[]{:S(2)}) collective-permute-start(f32[1,160,128]{2,1,0:T(8,128)S(1)} %get-tuple-element.24), channel_id=1, source_target_pairs={{8,0},{16,8},{24,16},{9,1},{17,9},{25,17},{10,2},{18,10},{26,18},{... | collective-permute-start | bytes 245768 | tf_op jit(solution)/shard_map/ppermute | solution.py:18
  21.6 12.3 %collective-permute-start.2 = (f32[1,160,128]{2,1,0:T(8,128)S(1)}, f32[1,160,128]{2,1,0:T(8,128)S(1)}, u32[]{:S(2)}, u32[]{:S(2)}) collective-permute-start(f32[1,160,128]{2,1,0:T(8,128)S(1)} %get-tuple-element.23), channel_id=1, source_target_pairs={{0,4},{1,5},{2,6},{3,7},{8,12},{9,13},{10,14},{11,15},{16,20},{17,... | collective-permute-start | bytes 245768 | tf_op jit(solution)/shard_map/ppermute | solution.py:15
  22.9 11.0 %collective-permute-start.3 = (f32[1,160,128]{2,1,0:T(8,128)S(1)}, f32[1,160,128]{2,1,0:T(8,128)S(1)}, u32[]{:S(2)}, u32[]{:S(2)}) collective-permute-start(f32[1,160,128]{2,1,0:T(8,128)S(1)} %get-tuple-element.22), channel_id=1, source_target_pairs={{4,0},{5,1},{6,2},{7,3},{12,8},{13,9},{14,10},{15,11},{20,16},{21,... | collective-permute-start | bytes 245768 | tf_op jit(solution)/shard_map/ppermute | solution.py:18
  26.9 7.1 %collective-permute-start.4 = (f32[1,160,128]{2,1,0:T(8,128)S(1)}, f32[1,160,128]{2,1,0:T(8,128)S(1)}, u32[]{:S(2)}, u32[]{:S(2)}) collective-permute-start(f32[1,160,128]{2,1,0:T(8,128)S(1)} %get-tuple-element.21), channel_id=1, source_target_pairs={{0,1},{1,2},{2,3},{4,5},{5,6},{6,7},{8,9},{9,10},{10,11},{12,13},{... | collective-permute-start | bytes 245768 | tf_op jit(solution)/shard_map/ppermute | solution.py:15
  32.0 5.8 collective-permute-start.5
  47.6 147.6 %all-reduce.7.cloned.1.call-start = ((), (), s32[]{:S(2)}) async-start(), calls=%async_computation.1 | async-start | bytes 4194304 | tf_op jit(solution)/shard_map/psum | solution.py:79
  107.6 149.0 %all-gather.3.cloned.1.call-start = ((), (), s32[]{:S(2)}) async-start(), calls=%async_computation.2 | async-start | bytes 2162688 | tf_op jit(solution)/shard_map/all_gather | solution.py:51
  200.3 193.4 %all-reduce.9.cloned.1.call-start = ((), (), s32[]{:S(2)}) async-start(), calls=%async_computation.3 | async-start | bytes 4194304 | tf_op jit(solution)/shard_map/psum | solution.py:79
  268.7 14.3 %collective-permute-start.6 = (f32[1,160,128]{2,1,0:T(8,128)S(1)}, f32[1,160,128]{2,1,0:T(8,128)S(1)}, u32[]{:S(2)}, u32[]{:S(2)}) collective-permute-start(f32[1,160,128]{2,1,0:T(8,128)S(1)} %get-tuple-element.19), channel_id=1, source_target_pairs={{0,8},{8,16},{16,24},{1,9},{9,17},{17,25},{2,10},{10,18},{18,26},{... | collective-permute-start | bytes 245768 | tf_op jit(solution)/shard_map/ppermute | solution.py:15
  271.1 13.9 %collective-permute-start.7 = (f32[1,160,128]{2,1,0:T(8,128)S(1)}, f32[1,160,128]{2,1,0:T(8,128)S(1)}, u32[]{:S(2)}, u32[]{:S(2)}) collective-permute-start(f32[1,160,128]{2,1,0:T(8,128)S(1)} %get-tuple-element.18), channel_id=1, source_target_pairs={{8,0},{16,8},{24,16},{9,1},{17,9},{25,17},{10,2},{18,10},{26,18},{... | collective-permute-start | bytes 245768 | tf_op jit(solution)/shard_map/ppermute | solution.py:18
  274.0 11.0 %collective-permute-start.8 = (f32[1,160,128]{2,1,0:T(8,128)S(1)}, f32[1,160,128]{2,1,0:T(8,128)S(1)}, u32[]{:S(2)}, u32[]{:S(2)}) collective-permute-start(f32[1,160,128]{2,1,0:T(8,128)S(1)} %get-tuple-element.17), channel_id=1, source_target_pairs={{0,4},{1,5},{2,6},{3,7},{8,12},{9,13},{10,14},{11,15},{16,20},{17,... | collective-permute-start | bytes 245768 | tf_op jit(solution)/shard_map/ppermute | solution.py:15
  275.3 9.7 %collective-permute-start.9 = (f32[1,160,128]{2,1,0:T(8,128)S(1)}, f32[1,160,128]{2,1,0:T(8,128)S(1)}, u32[]{:S(2)}, u32[]{:S(2)}) collective-permute-start(f32[1,160,128]{2,1,0:T(8,128)S(1)} %get-tuple-element.16), channel_id=1, source_target_pairs={{4,0},{5,1},{6,2},{7,3},{12,8},{13,9},{14,10},{15,11},{20,16},{21,... | collective-permute-start | bytes 245768 | tf_op jit(solution)/shard_map/ppermute | solution.py:18
  304.9 13.7 %collective-permute-start.12 = (f32[1,160,128]{2,1,0:T(8,128)S(1)}, f32[1,160,128]{2,1,0:T(8,128)S(1)}, u32[]{:S(2)}, u32[]{:S(2)}) collective-permute-start(f32[1,160,128]{2,1,0:T(8,128)S(1)} %get-tuple-element.13), channel_id=1, source_target_pairs={{0,8},{8,16},{16,24},{1,9},{9,17},{17,25},{2,10},{10,18},{18,26},{... | collective-permute-start | bytes 245768 | tf_op jit(solution)/shard_map/ppermute | solution.py:15
  307.4 13.1 %collective-permute-start.13 = (f32[1,160,128]{2,1,0:T(8,128)S(1)}, f32[1,160,128]{2,1,0:T(8,128)S(1)}, u32[]{:S(2)}, u32[]{:S(2)}) collective-permute-start(f32[1,160,128]{2,1,0:T(8,128)S(1)} %get-tuple-element.12), channel_id=1, source_target_pairs={{8,0},{16,8},{24,16},{9,1},{17,9},{25,17},{10,2},{18,10},{26,18},{... | collective-permute-start | bytes 245768 | tf_op jit(solution)/shard_map/ppermute | solution.py:18
  310.2 10.4 %collective-permute-start.14 = (f32[1,160,128]{2,1,0:T(8,128)S(1)}, f32[1,160,128]{2,1,0:T(8,128)S(1)}, u32[]{:S(2)}, u32[]{:S(2)}) collective-permute-start(f32[1,160,128]{2,1,0:T(8,128)S(1)} %get-tuple-element.11), channel_id=1, source_target_pairs={{0,4},{1,5},{2,6},{3,7},{8,12},{9,13},{10,14},{11,15},{16,20},{17,... | collective-permute-start | bytes 245768 | tf_op jit(solution)/shard_map/ppermute | solution.py:15
  311.5 9.2 %collective-permute-start.15 = (f32[1,160,128]{2,1,0:T(8,128)S(1)}, f32[1,160,128]{2,1,0:T(8,128)S(1)}, u32[]{:S(2)}, u32[]{:S(2)}) collective-permute-start(f32[1,160,128]{2,1,0:T(8,128)S(1)} %get-tuple-element.10), channel_id=1, source_target_pairs={{4,0},{5,1},{6,2},{7,3},{12,8},{13,9},{14,10},{15,11},{20,16},{21,... | collective-permute-start | bytes 245768 | tf_op jit(solution)/shard_map/ppermute | solution.py:18
  334.2 146.9 %all-reduce.11.cloned.1.call-start = ((), (), s32[]{:S(2)}) async-start(), calls=%async_computation.4 | async-start | bytes 4194304 | tf_op jit(solution)/shard_map/psum | solution.py:79
  393.7 148.9 %all-gather.5.cloned.1.call-start = ((), (), s32[]{:S(2)}) async-start(), calls=%async_computation.5 | async-start | bytes 2162688 | tf_op jit(solution)/shard_map/all_gather | solution.py:51
  558.6 15.4 %collective-permute-start.18 = (f32[1,160,128]{2,1,0:T(8,128)S(1)}, f32[1,160,128]{2,1,0:T(8,128)S(1)}, u32[]{:S(2)}, u32[]{:S(2)}) collective-permute-start(f32[1,160,128]{2,1,0:T(8,128)S(1)} %get-tuple-element.7), channel_id=1, source_target_pairs={{0,8},{8,16},{16,24},{1,9},{9,17},{17,25},{2,10},{10,18},{18,26},{... | collective-permute-start | bytes 245768 | tf_op jit(solution)/shard_map/ppermute | solution.py:15
  561.9 14.1 %collective-permute-start.19 = (f32[1,160,128]{2,1,0:T(8,128)S(1)}, f32[1,160,128]{2,1,0:T(8,128)S(1)}, u32[]{:S(2)}, u32[]{:S(2)}) collective-permute-start(f32[1,160,128]{2,1,0:T(8,128)S(1)} %get-tuple-element.6), channel_id=1, source_target_pairs={{8,0},{16,8},{24,16},{9,1},{17,9},{25,17},{10,2},{18,10},{26,18},{... | collective-permute-start | bytes 245768 | tf_op jit(solution)/shard_map/ppermute | solution.py:18
  564.8 11.2 %collective-permute-start.20 = (f32[1,160,128]{2,1,0:T(8,128)S(1)}, f32[1,160,128]{2,1,0:T(8,128)S(1)}, u32[]{:S(2)}, u32[]{:S(2)}) collective-permute-start(f32[1,160,128]{2,1,0:T(8,128)S(1)} %get-tuple-element.5), channel_id=1, source_target_pairs={{0,4},{1,5},{2,6},{3,7},{8,12},{9,13},{10,14},{11,15},{16,20},{17,... | collective-permute-start | bytes 245768 | tf_op jit(solution)/shard_map/ppermute | solution.py:15
  566.3 9.7 %collective-permute-start.21 = (f32[1,160,128]{2,1,0:T(8,128)S(1)}, f32[1,160,128]{2,1,0:T(8,128)S(1)}, u32[]{:S(2)}, u32[]{:S(2)}) collective-permute-start(f32[1,160,128]{2,1,0:T(8,128)S(1)} %get-tuple-element.4), channel_id=1, source_target_pairs={{4,0},{5,1},{6,2},{7,3},{12,8},{13,9},{14,10},{15,11},{20,16},{21,... | collective-permute-start | bytes 245768 | tf_op jit(solution)/shard_map/ppermute | solution.py:18
  (12 other events, 138.8 us)
Sparse Core Ops, SparseCore 0:
  47.8 59.7 all-reduce.4
  110.0 85.2 all-reduce.6
  200.4 56.2 all-gather.2
  334.4 59.2 all-reduce.8
  395.9 85.2 all-reduce.10
  486.3 56.2 all-gather.4
